TPU v7x, 32 devices: a whole 2x2x4 slice. The times are simulated.
32 devices in a mesh: lon: 4 (over y, x), lat: 8 (over z, core).
Axes of the slice: x: 2, y: 2, z: 4, core: 2. Of those that a mesh axis runs over, the one named last changes fastest.
Arguments:
- ocean_field: bfloat16 [256, 1024, 128], P('lon', 'lat'), may hold values from -6 to 6
- wet_tiles: int32 [4, 16], P('lon', 'lat'), may hold values from 0 to 1
- conv_weight: bfloat16 [2, 7, 7, 128], replicated, may hold values from -0.875 to 0.875
- norm_gain: float32 [2, 128], replicated, may hold values from 0.1 to 1.9
- norm_bias: float32 [2, 128], replicated, may hold values from -3 to 3
- inner_weight: bfloat16 [2, 128, 256], replicated, may hold values from -0.5 to 0.5
- inner_bias: float32 [2, 256], replicated, may hold values from -3 to 3
- outer_weight: bfloat16 [2, 256, 128], replicated, may hold values from -0.375 to 0.375
- outer_bias: float32 [2, 128], replicated, may hold values from -3 to 3
Outputs:
- updated_field: bfloat16 [256, 1024, 128], P('lon', 'lat')
All inputs are finite; a program needn't handle non-finite values.
Results may differ from a plain program's by a relative error of at most 0.0069.
Values may be sent and summed in bfloat16 or wider, within the bound.
No kernel may reach another device: no remote copies, remote signals or barrier semaphores. Data moves between devices by JAX's collectives and lax.ppermute only.
A program may use at most 64 MiB of HBM per device.

v0:
```python
import functools

import jax
import jax.numpy as jnp
from jax import lax
from jax.experimental import pallas as pl
from jax.experimental.pallas import tpu as pltpu
from jax.sharding import PartitionSpec as P

PHASE_I = 8
PHASE_J = 2
PHASES = PHASE_I * PHASE_J
SEG = 16
STRIPS = 16
LEFT = 8
REACH = 3
RIM = 2 * REACH
LANES = 128
WIDE = 256
CHUNKS = 8
INNER_MIB = 20
OUTER_MIB = 26
WHOLE_VMEM = 67043328


def swap_segments(parts, back=False):
    parts = list(parts)
    lane = lax.broadcasted_iota(jnp.int32, parts[0].shape, 1)
    for dist in (1, 2, 4) if back else (4, 2, 1):
        low_side = (lane // (SEG * dist)) % 2 == 0
        turn = LANES - SEG * dist if back else SEG * dist
        for p in range(8):
            if p & dist:
                continue
            low, high = parts[p], parts[p + dist]
            moved = pltpu.roll(jnp.where(low_side, high, low), turn, 1)
            parts[p] = jnp.where(low_side, low, moved)
            parts[p + dist] = jnp.where(low_side, moved, high)
    return parts


def lane_slot(g, p):
    p1, p2, p4 = p & 1, p >> 1 & 1, p >> 2 & 1
    high = p4 ^ ((g >> 1) & (1 - p2))
    return ((high * 2 + p2 + (g & (1 - p1))) & 3) * 2 + p1


def band_body(conv_ref, band_ref, taps_ref, rows_ref):
    f32 = jnp.float32
    g = pl.program_id(0)

    @pl.when(g == 0)
    def _():
        taps_ref[...] = jnp.zeros(taps_ref.shape, f32)
        taps_ref[7:14, 8:15, :] = conv_ref[...].astype(f32)

        def tap_rows(q, carry):
            for half in range(2):
                parts = []
                for p in range(8):
                    pi, pj = (half * 8 + p) // 2, (half * 8 + p) % 2
                    parts.append(taps_ref[q - pi + 7, pl.ds(8 - pj, 8), :])
                for group, part in enumerate(swap_segments(parts)):
                    rows_ref[group, q, half] = part
            return carry

        lax.fori_loop(0, 2 * PHASE_I, tap_rows, 0, unroll=4)

    lane = lax.broadcasted_iota(jnp.int32, (SEG, LANES), 1)
    own = lax.broadcasted_iota(jnp.int32, (SEG, LANES), 0) == lane % SEG
    for kb in range(2):
        for p in range(PHASES):
            slot = (p >> 3) * 8 + lane_slot(g, p & 7)
            at = pl.ds(pl.multiple_of(slot * SEG, SEG), SEG)
            for ub in range(4):
                r = 2 * ub + (p & 1)
                for half in range(2):
                    row = rows_ref[g, kb * PHASE_I + (p >> 1), half, r : r + 1, :]
                    band_ref[0, kb * 4 + ub, half, at, :] = jnp.where(
                        own, jnp.broadcast_to(row, (SEG, LANES)), 0.0
                    ).astype(jnp.bfloat16)


def band_call(kernels, layer):
    groups = kernels.shape[3] // SEG
    return pl.pallas_call(
        band_body,
        grid=(groups,),
        out_shape=jax.ShapeDtypeStruct((groups, CHUNKS, 2, WIDE, LANES), jnp.bfloat16),
        in_specs=[pl.BlockSpec((None,) + kernels.shape[1:], lambda g: (layer, 0, 0, 0))],
        out_specs=pl.BlockSpec((1, CHUNKS, 2, WIDE, LANES), lambda g: (g, 0, 0, 0, 0)),
        scratch_shapes=[
            pltpu.VMEM((24, 24, LANES), jnp.float32),
            pltpu.VMEM((groups, 2 * PHASE_I, 2, 8, LANES), jnp.float32),
        ],
        compiler_params=pltpu.CompilerParams(vmem_limit_bytes=16 << 20),
        cost_estimate=pl.CostEstimate(
            flops=16 << 20, bytes_accessed=groups * CHUNKS * WIDE * WIDE * 2, transcendentals=0
        ),
        name="bands",
    )(kernels)


def rim_cols_body(wet_hbm, state_hbm, head_ref, tail_ref, wet_ref, left_ref, right_ref, sems, *, tile):
    f32 = jnp.float32
    _, chunk, channels = left_ref.shape
    width = state_hbm.shape[1]
    copies = [
        pltpu.make_async_copy(wet_hbm, wet_ref, sems.at[0]),
        pltpu.make_async_copy(state_hbm.at[:, 0:chunk, :], left_ref, sems.at[1]),
        pltpu.make_async_copy(state_hbm.at[:, width - chunk : width, :], right_ref, sems.at[2]),
    ]
    for copy in copies:
        copy.start()
    for copy in copies:
        copy.wait()
    tiles_i, tiles_j = wet_ref.shape
    for cols_ref, out_ref, tj, first in (
        (left_ref, head_ref, 0, 0),
        (right_ref, tail_ref, tiles_j - 1, chunk - RIM),
    ):
        for ti in range(tiles_i):
            wet = wet_ref[ti, tj] > 0
            at = slice(ti * tile, (ti + 1) * tile)
            piece = cols_ref[at].astype(f32)
            kept = jnp.where(wet, piece[:, first : first + RIM], 0.0)
            flag = jnp.full((tile, 1, channels), jnp.where(wet, 1.0, 0.0), f32)
            out_ref[at] = jnp.concatenate([kept, flag], axis=1).astype(jnp.bfloat16)


def rim_cols_call(wet, state, tile):
    height, _, channels = state.shape
    shape = jax.ShapeDtypeStruct((height, RIM + 1, channels), jnp.bfloat16)
    vmem = pl.BlockSpec(memory_space=pltpu.VMEM)
    hbm = pl.BlockSpec(memory_space=pltpu.HBM)
    return pl.pallas_call(
        functools.partial(rim_cols_body, tile=tile),
        out_shape=[shape, shape],
        in_specs=[hbm, hbm],
        out_specs=[vmem, vmem],
        scratch_shapes=[
            pltpu.SMEM(wet.shape, jnp.int32),
            pltpu.VMEM((height, 8, channels), state.dtype),
            pltpu.VMEM((height, 8, channels), state.dtype),
            pltpu.SemaphoreType.DMA((3,)),
        ],
        compiler_params=pltpu.CompilerParams(vmem_limit_bytes=WHOLE_VMEM),
        name="rim_cols",
    )(wet, state)


def rim_rows_body(wet_ref, state_ref, west_ref, east_ref, head_ref, tail_ref, *, tile):
    f32 = jnp.float32
    bf16 = jnp.bfloat16
    height, width, channels = state_ref.shape
    for out_ref, ti, first in ((head_ref, 0, 0), (tail_ref, wet_ref.shape[0] - 1, height - RIM)):
        out_ref[:, 0:LEFT, :] = jnp.zeros((RIM + 1, LEFT, channels), bf16)
        out_ref[:, LEFT + width :, :] = jnp.zeros((RIM + 1, LEFT, channels), bf16)
        for side_ref, at in ((west_ref, LEFT - RIM), (east_ref, LEFT + width)):
            side = side_ref[first : first + RIM].astype(f32)
            out_ref[0:RIM, at : at + RIM, :] = side[:, 0:RIM].astype(bf16)
            out_ref[RIM, at : at + RIM, :] = jnp.broadcast_to(
                side[0, RIM : RIM + 1], (RIM, channels)
            ).astype(bf16)
        for tj in range(width // tile):
            wet = wet_ref[ti, tj] > 0
            at = slice(LEFT + tj * tile, LEFT + (tj + 1) * tile)
            for r in range(RIM):
                piece = state_ref[first + r, tj * tile : (tj + 1) * tile, :].astype(f32)
                out_ref[r, at, :] = jnp.where(wet, piece, 0.0).astype(bf16)
            out_ref[RIM, at, :] = jnp.full(
                (tile, channels), jnp.where(wet, 1.0, 0.0), f32
            ).astype(bf16)


def rim_rows_call(wet, state, west, east, tile):
    _, width, channels = state.shape
    shape = jax.ShapeDtypeStruct((RIM + 1, width + 2 * LEFT, channels), jnp.bfloat16)
    vmem = pl.BlockSpec(memory_space=pltpu.VMEM)
    return pl.pallas_call(
        functools.partial(rim_rows_body, tile=tile),
        out_shape=[shape, shape],
        in_specs=[pl.BlockSpec(memory_space=pltpu.SMEM)] + [vmem] * 3,
        out_specs=[vmem, vmem],
        compiler_params=pltpu.CompilerParams(vmem_limit_bytes=8 << 20),
        name="rim_rows",
    )(wet, state, west, east)


def prepare_weights(inner_ref, inner_bias_ref, outer_ref, inner_wide_ref, outer_half_ref, layers):
    f32 = jnp.float32
    bf16 = jnp.bfloat16
    _, channels, hidden_dim = inner_ref.shape
    which = lax.broadcasted_iota(jnp.int32, (channels, hidden_dim), 0)
    for index in layers:
        inner_wide_ref[index, 0:channels, :] = inner_ref[index]
        rest = inner_bias_ref[index : index + 1]
        tail = jnp.zeros((channels, hidden_dim), f32)
        for k in range(3):
            part = rest.astype(bf16).astype(f32)
            rest = rest - part
            tail = jnp.where(which == k, part, tail)
        inner_wide_ref[index, channels : 2 * channels, :] = tail.astype(bf16)
        outer_half_ref[index] = (outer_ref[index].astype(f32) * 0.5).astype(bf16)


def prepare_moments(average_ref, center_ref, channels):
    row = lax.broadcasted_iota(jnp.int32, (WIDE, WIDE), 0)
    col = lax.broadcasted_iota(jnp.int32, (WIDE, WIDE), 1)
    share = jnp.where(row // channels == col // channels, 1.0 / channels, 0.0)
    average_ref[...] = share.astype(jnp.bfloat16)
    center_ref[...] = (jnp.where(row == col, 1.0, 0.0) - share).astype(jnp.bfloat16)


def fill_wide(wide_ref, wet_ref, state_ref, west_ref, east_ref, rows, at, tile):
    f32 = jnp.float32
    _, width, _ = state_ref.shape
    first, last = rows
    here = slice(at, at + last - first)
    wide_ref[here, LEFT - RIM : LEFT, :] = west_ref[first:last, 0:RIM, :].astype(f32)
    wide_ref[here, LEFT + width : LEFT + width + RIM, :] = east_ref[first:last, 0:RIM, :].astype(f32)

    def widen(k, carry):
        for tj in range(width // tile):
            wet = wet_ref[(first + k) // tile, tj] > 0
            piece = state_ref[first + k, tj * tile : (tj + 1) * tile, :].astype(f32)
            wide_ref[at + k, LEFT + tj * tile : LEFT + (tj + 1) * tile, :] = jnp.where(
                wet, piece, 0.0
            )
        return carry

    lax.fori_loop(0, last - first, widen, 0, unroll=4)


def fill_mask(mask_ref, wets_ref, region, steps):
    for t in range(steps):
        wets_ref[region, t] = mask_ref[region, pl.ds(LEFT - REACH + t, STRIPS, stride=steps), :]


def fill_inner_masks(mask_ref, wets_ref, wet_ref, west_ref, east_ref, width, steps, tile):
    f32 = jnp.float32
    tiles_i, tiles_j = wet_ref.shape
    channels = west_ref.shape[2]
    for region in range(1, tiles_i + 1):
        for tj in range(tiles_j):
            flag = jnp.where(wet_ref[region - 1, tj] > 0, 1.0, 0.0)
            mask_ref[region, LEFT + tj * tile : LEFT + (tj + 1) * tile, :] = jnp.full(
                (tile, channels), flag, f32
            )
        edge = (region - 1) * tile
        for side_ref, at in ((west_ref, LEFT - REACH), (east_ref, LEFT + width)):
            mask_ref[region, at : at + REACH, :] = jnp.broadcast_to(
                side_ref[edge, RIM : RIM + 1, :].astype(f32), (REACH, channels)
            )
        fill_mask(mask_ref, wets_ref, region, steps)


def run_layer(
    index,
    source_ref,
    band_ref,
    start,
    steps,
    sources,
    picks,
    weights,
    packed,
    store,
    finish=None,
):
    gain_ref, bias_ref, outer_bias_ref, inner_wide_ref, outer_half_ref, average_ref, center_ref = weights
    phased_ref, grouped_ref, cells_ref, normed_ref = packed
    bf16 = jnp.bfloat16
    f32 = jnp.float32
    channels = gain_ref.shape[1]
    groups = channels // SEG
    pairs = steps // PHASE_J
    blocks = sum(n for _, n in picks[0])
    count = PHASE_I * pairs * STRIPS
    gain = jnp.concatenate([gain_ref[index : index + 1]] * 2, axis=1)
    shift = jnp.concatenate([bias_ref[index : index + 1]] * 2, axis=1)
    bias_lanes = jnp.where(
        lax.broadcasted_iota(jnp.int32, (count, channels), 1) < 3, 1.0, 0.0
    ).astype(bf16)

    def to_phases(blk, carry):
        for u in range(pairs + 3):
            for half in range(2):
                parts = []
                for p in range(8):
                    pi, pj = (half * 8 + p) // 2, (half * 8 + p) % 2
                    strip = source_ref[
                        blk * PHASE_I + pi, pl.ds(start + 2 * u + pj, STRIPS, stride=steps), :
                    ]
                    parts.append(strip.astype(bf16))
                for g, part in enumerate(swap_segments(parts)):
                    phased_ref[g, half, blk, u] = part
        return carry

    lax.fori_loop(0, sources, to_phases, 0)

    def convolve(g, carry):
        slabs = []
        mats = []
        for kb in range(2):
            for ub in range(4):
                for half in range(2):
                    runs = [
                        phased_ref[g, half, first : first + n, ub : ub + pairs].reshape(
                            n * pairs * STRIPS, LANES
                        )
                        for first, n in picks[kb]
                    ]
                    slabs.append(runs[0] if len(runs) == 1 else jnp.concatenate(runs, axis=0))
                band = band_ref.at[g, kb * 4 + ub]
                mats.append(jnp.concatenate([band[0], band[1]], axis=1))
        total = jnp.dot(
            jnp.concatenate(slabs, axis=1),
            jnp.concatenate(mats, axis=0),
            preferred_element_type=f32,
        ).astype(bf16)
        for half in range(2):
            grouped_ref[g, half, 0:blocks, 0:pairs] = total[
                :, half * LANES : (half + 1) * LANES
            ].reshape(blocks, pairs, STRIPS, LANES)
        return carry

    lax.fori_loop(0, groups, convolve, 0, unroll=4)

    def to_cells(blk):
        for v in range(pairs):
            for half in range(2):
                parts = swap_segments(
                    [grouped_ref[g, half, blk, v] for g in range(groups)], back=True
                )
                for p in range(8):
                    pi, pj = (half * 8 + p) // 2, (half * 8 + p) % 2
                    cells_ref[pj, pi, v] = parts[p]

    def normalize():
        conv = jnp.concatenate(
            [cells_ref[pj, :, 0:pairs].reshape(count, channels) for pj in range(PHASE_J)],
            axis=1,
        )
        centered = jnp.dot(conv, center_ref[...], preferred_element_type=f32)
        var = jnp.dot(
            (centered * centered).astype(bf16), average_ref[...], preferred_element_type=f32
        )
        normed = (centered * lax.rsqrt(var + 1e-06) * gain + shift).astype(bf16)
        for pj in range(PHASE_J):
            normed_ref[pj, 0:count] = normed[:, pj * channels : (pj + 1) * channels]

    def mix(blk, carry):
        if finish is not None:
            finish(jnp.maximum(blk - 1, 0))
        for pj in range(PHASE_J):
            pre = jnp.dot(
                jnp.concatenate([normed_ref[pj, 0:count], bias_lanes], axis=1),
                inner_wide_ref[index],
                preferred_element_type=f32,
            )
            hidden = (pre * (1.0 + lax.erf(pre * 0.7071067811865476))).astype(bf16)
            branch = (
                jnp.dot(hidden, outer_half_ref[index], preferred_element_type=f32)
                + outer_bias_ref[index : index + 1]
            ).reshape(PHASE_I, pairs, STRIPS, channels)
            for pi in range(PHASE_I):
                for v in range(pairs):
                    store(blk, pi, 2 * v + pj, branch[pi, v])
        normalize()
        to_cells(jnp.minimum(blk + 2, blocks - 1))
        return carry

    to_cells(0)
    normalize()
    to_cells(1)
    lax.fori_loop(0, blocks, mix, 0)
    if finish is not None:
        finish(blocks - 1)


def region_of(r, height, tile):
    region = jnp.int32(0)
    for bound in range(REACH, REACH + height + 1, tile):
        region += (r >= bound).astype(jnp.int32)
    return region


def inner_body(
    wet_ref,
    state_ref,
    west_ref,
    east_ref,
    band_ref,
    gain_ref,
    bias_ref,
    inner_ref,
    inner_bias_ref,
    outer_ref,
    outer_bias_ref,
    out_ref,
    wide_ref,
    mask_ref,
    wets_ref,
    average_ref,
    center_ref,
    inner_wide_ref,
    outer_half_ref,
    *,
    tile,
    steps,
    **packed,
):
    height, width, channels = state_ref.shape
    blocks = out_ref.shape[0] // PHASE_I
    f32 = jnp.float32
    top = PHASE_I - RIM
    wide_ref[:, LEFT + width :, :] = jnp.zeros(
        (wide_ref.shape[0], wide_ref.shape[1] - LEFT - width, channels), f32
    )
    fill_wide(
        wide_ref, wet_ref, state_ref, west_ref, east_ref, (top, top + wide_ref.shape[0]), 0, tile
    )
    mask_ref[...] = jnp.zeros(mask_ref.shape, f32)
    fill_inner_masks(mask_ref, wets_ref, wet_ref, west_ref, east_ref, width, steps, tile)
    prepare_weights(inner_ref, inner_bias_ref, outer_ref, inner_wide_ref, outer_half_ref, (0,))
    prepare_moments(average_ref, center_ref, channels)

    def store(blk, pi, t, branch):
        k = blk * PHASE_I + pi
        at = pl.ds(LEFT - REACH + t, STRIPS, stride=steps)
        region = region_of(k + PHASE_I, height, tile)
        out_ref[k, at, :] = (wide_ref[k + REACH, at, :] + branch) * wets_ref[region, t]

    run_layer(
        0,
        wide_ref,
        band_ref,
        LEFT - RIM,
        steps,
        blocks + 1,
        [[(kb, blocks)] for kb in range(2)],
        (gain_ref, bias_ref, outer_bias_ref, inner_wide_ref, outer_half_ref, average_ref, center_ref),
        tuple(packed[k] for k in PACKED),
        store,
    )


def outer_body(
    wet_ref,
    state_ref,
    top_ref,
    bottom_ref,
    west_ref,
    east_ref,
    band_a_ref,
    band_b_ref,
    part_ref,
    gain_ref,
    bias_ref,
    inner_ref,
    inner_bias_ref,
    outer_ref,
    outer_bias_ref,
    out_ref,
    wide_ref,
    second_ref,
    mask_ref,
    wets_ref,
    branch_ref,
    average_ref,
    center_ref,
    inner_wide_ref,
    outer_half_ref,
    sem,
    *,
    tile,
    steps,
    **packed,
):
    height, width, channels = state_ref.shape
    bf16 = jnp.bfloat16
    f32 = jnp.float32
    inner_rows = part_ref.shape[0]
    low = PHASE_I + inner_rows
    copy = pltpu.make_async_copy(part_ref, second_ref.at[PHASE_I:low], sem)
    copy.start()

    cut = 2 * PHASE_I
    ends = cut + height + RIM - low
    wide_ref[:, LEFT + width :, :] = jnp.zeros(
        (wide_ref.shape[0], wide_ref.shape[1] - LEFT - width, channels), f32
    )
    wide_ref[ends + RIM :] = jnp.zeros((wide_ref.shape[0] - ends - RIM,) + wide_ref.shape[1:], f32)
    span = slice(0, width + 2 * LEFT)
    wide_ref[0:RIM, span, :] = top_ref[0:RIM].astype(f32)
    wide_ref[ends : ends + RIM, span, :] = bottom_ref[0:RIM].astype(f32)
    fill_wide(wide_ref, wet_ref, state_ref, west_ref, east_ref, (0, cut - RIM), RIM, tile)
    fill_wide(wide_ref, wet_ref, state_ref, west_ref, east_ref, (low - RIM, height), cut, tile)
    mask_ref[...] = jnp.zeros(mask_ref.shape, f32)
    fill_inner_masks(mask_ref, wets_ref, wet_ref, west_ref, east_ref, width, steps, tile)
    for region, rim_ref in ((0, top_ref), (mask_ref.shape[0] - 1, bottom_ref)):
        mask_ref[region, span, :] = rim_ref[RIM].astype(f32)
        fill_mask(mask_ref, wets_ref, region, steps)
    prepare_weights(inner_ref, inner_bias_ref, outer_ref, inner_wide_ref, outer_half_ref, (0, 1))
    prepare_moments(average_ref, center_ref, channels)
    weights = (
        gain_ref,
        bias_ref,
        outer_bias_ref,
        inner_wide_ref,
        outer_half_ref,
        average_ref,
        center_ref,
    )
    packed = tuple(packed[k] for k in PACKED)

    def store_first(blk, pi, t, branch):
        later = (blk > 0).astype(jnp.int32)
        r = blk * PHASE_I + pi + later * inner_rows
        at = pl.ds(LEFT - REACH + t, STRIPS, stride=steps)
        base = wide_ref[(blk + later) * PHASE_I + pi + REACH, at, :]
        second_ref[r, at, :] = (base + branch) * wets_ref[region_of(r, height, tile), t]

    tails = wide_ref.shape[0] // PHASE_I - 3
    run_layer(
        0,
        wide_ref,
        band_a_ref,
        LEFT - RIM,
        steps,
        tails + 3,
        [[(kb, 1), (2 + kb, tails)] for kb in range(2)],
        weights,
        packed,
        store_first,
    )
    copy.wait()
    steps_b = width // STRIPS
    blocks = height // PHASE_I

    def store_second(blk, pi, t, branch):
        branch_ref[pi, t * STRIPS : (t + 1) * STRIPS, :] = branch

    def finish(blk):
        for pi in range(PHASE_I):
            i = blk * PHASE_I + pi
            for s in range(0, STRIPS, 2):
                wet = wet_ref[i // tile, s * steps_b // tile] > 0
                delta = jnp.concatenate(
                    [branch_ref[pi, pl.ds(s + k, steps_b, stride=STRIPS), :] for k in range(2)],
                    axis=0,
                )
                base = second_ref[i + REACH, LEFT + s * steps_b : LEFT + (s + 2) * steps_b, :]
                out_ref[i, s * steps_b : (s + 2) * steps_b, :] = jnp.where(
                    wet, base + delta, 0.0
                ).astype(bf16)

    run_layer(
        1,
        second_ref,
        band_b_ref,
        LEFT - REACH,
        steps_b,
        blocks + 1,
        [[(kb, blocks)] for kb in range(2)],
        weights,
        packed,
        store_second,
        finish,
    )


PACKED = ("phased_ref", "grouped_ref", "cells_ref", "normed_ref")


def in_kernel(body, groups, sources, blocks, pairs, **options):
    packed = dict(
        phased_ref=pltpu.VMEM((groups, 2, sources, pairs + 3, STRIPS, LANES), jnp.bfloat16),
        grouped_ref=pltpu.VMEM((groups, 2, blocks, pairs, STRIPS, LANES), jnp.bfloat16),
        cells_ref=pltpu.VMEM((PHASE_J, PHASE_I, pairs, STRIPS, LANES), jnp.bfloat16),
        normed_ref=pltpu.VMEM((PHASE_J, PHASE_I * pairs * STRIPS, LANES), jnp.bfloat16),
    )

    def run(*refs):
        pl.run_scoped(functools.partial(body, *refs, **options), **packed)

    return run


def plan(state):
    height, width, channels = state.shape
    blocks = pl.cdiv(height + 2 * REACH, PHASE_I)
    steps = PHASE_J * pl.cdiv(width + 2 * REACH, STRIPS * PHASE_J)
    inner = (height + RIM - 2 * PHASE_I) // PHASE_I
    assert channels == LANES and width == STRIPS * 8 and height % PHASE_I == 0 and inner > 1
    return blocks, steps, inner


def shared_scratch(weights, regions, span, steps):
    channels, hidden = weights[2].shape[1:]
    return (
        [
            pltpu.VMEM((regions, span, channels), jnp.float32),
            pltpu.VMEM((regions, steps, STRIPS, channels), jnp.float32),
        ],
        [
            pltpu.VMEM((WIDE, WIDE), jnp.bfloat16),
            pltpu.VMEM((WIDE, WIDE), jnp.bfloat16),
            pltpu.VMEM((2, 2 * channels, hidden), jnp.bfloat16),
            pltpu.VMEM((2, hidden, channels), jnp.bfloat16),
        ],
    )


def inner_call(wet, state, west, east, band, weights, tile):
    height, _, channels = state.shape
    _, steps, inner = plan(state)
    span = LEFT + STRIPS * steps
    vmem = pl.BlockSpec(memory_space=pltpu.VMEM)
    masks, mats = shared_scratch(weights, height // tile + 2, span, steps)
    cells = PHASE_I * inner * STRIPS * steps
    return pl.pallas_call(
        in_kernel(
            inner_body, channels // SEG, inner + 1, inner, steps // PHASE_J, tile=tile, steps=steps
        ),
        out_shape=jax.ShapeDtypeStruct((PHASE_I * inner, span, channels), jnp.float32),
        in_specs=[pl.BlockSpec(memory_space=pltpu.SMEM)] + [vmem] * 10,
        out_specs=vmem,
        scratch_shapes=[pltpu.VMEM((PHASE_I * (inner + 1), span, channels), jnp.float32)]
        + masks
        + mats,
        compiler_params=pltpu.CompilerParams(vmem_limit_bytes=INNER_MIB << 20),
        cost_estimate=pl.CostEstimate(
            flops=cells * channels * 2000, bytes_accessed=cells * channels * 8, transcendentals=0
        ),
        name="inner_blocks",
    )(wet, state, west, east, band, *weights)


def outer_call(wet, state, top, bottom, west, east, bands, part, weights, tile):
    height, width, channels = state.shape
    blocks, steps, inner = plan(state)
    span = LEFT + STRIPS * steps
    vmem = pl.BlockSpec(memory_space=pltpu.VMEM)
    masks, mats = shared_scratch(weights, height // tile + 2, span, steps)
    tails = blocks - 1 - inner
    return pl.pallas_call(
        in_kernel(
            outer_body,
            channels // SEG,
            height // PHASE_I + 1,
            height // PHASE_I,
            steps // PHASE_J,
            tile=tile,
            steps=steps,
        ),
        out_shape=jax.ShapeDtypeStruct(state.shape, jnp.bfloat16),
        in_specs=[pl.BlockSpec(memory_space=pltpu.SMEM)] + [vmem] * 14,
        out_specs=vmem,
        scratch_shapes=[
            pltpu.VMEM((PHASE_I * (tails + 3), span, channels), jnp.float32),
            pltpu.VMEM((PHASE_I * blocks, span, channels), jnp.float32),
        ]
        + masks
        + [pltpu.VMEM((PHASE_I, width, channels), jnp.float32)]
        + mats
        + [pltpu.SemaphoreType.DMA],
        compiler_params=pltpu.CompilerParams(vmem_limit_bytes=OUTER_MIB << 20),
        name="outer_blocks",
    )(wet, state, top, bottom, west, east, *bands, part, *weights)


def shift_pair(head, tail, axis, closed):
    count = lax.axis_size(axis)
    ends = count if closed else count - 1
    before = lax.ppermute(tail, axis, [(i, (i + 1) % count) for i in range(ends)])
    after = lax.ppermute(head, axis, [((i + 1) % count, i) for i in range(ends)])
    return before, after


def per_device(
    ocean_field,
    wet_tiles,
    conv_weight,
    norm_gain,
    norm_bias,
    inner_weight,
    inner_bias,
    outer_weight,
    outer_bias,
):
    tile = ocean_field.shape[0] // wet_tiles.shape[0]
    cols = rim_cols_call(wet_tiles, ocean_field, tile)
    west, east = shift_pair(*cols, "lat", False)
    rows = rim_rows_call(wet_tiles, ocean_field, west, east, tile)
    top, bottom = shift_pair(*rows, "lon", True)
    bands = []
    for layer in range(conv_weight.shape[0]):
        bands.append(band_call(conv_weight, layer))
    weights = (norm_gain, norm_bias, inner_weight, inner_bias, outer_weight, outer_bias)
    part = inner_call(wet_tiles, ocean_field, west, east, bands[0], weights, tile)
    return outer_call(wet_tiles, ocean_field, top, bottom, west, east, bands, part, weights, tile)


def solution(mesh):
    return jax.shard_map(
        per_device,
        mesh=mesh,
        in_specs=(P("lon", "lat", None), P("lon", "lat"), P(), P(), P(), P(), P(), P(), P()),
        out_specs=P("lon", "lat", None),
        check_vma=False,
    )
```

profile of v0, /device:TPU:1, one launch (start us, length us, event | category | flops | bytes accessed | tf_op | source)
XLA Modules:
  0.0 63.8 jit_solution(16523841776389175134)
XLA Ops:
  0.0 1.8 %rim_cols.1 = (bf16[64,7,128]{2,1,0:T(8,128)(2,1)}, bf16[64,7,128]{2,1,0:T(8,128)(2,1)}) custom-call(s32[1,2]{1,0:T(1,128)} %refs_0_.3, bf16[64,128,128]{2,1,0:T(8,128)(2,1)} %refs_1_.3), custom_call_target="tpu_custom_call" | custom-call | tf_op jit(solution)/shard_map/rim_cols/pallas_call | solution.py:136
  1.8 4.6 %collective-permute-start = (bf16[64,7,128]{2,1,0:T(8,128)(2,1)}, bf16[64,7,128]{2,1,0:T(8,128)(2,1)S(1)}, u32[]{:S(2)}, u32[]{:S(2)}) collective-permute-start(bf16[64,7,128]{2,1,0:T(8,128)(2,1)} %get-tuple-element.9), channel_id=1, source_target_pairs={{0,1},{1,2},{2,3},{3,4},{4,5},{5,6},{6,7},{8,9},{9,10},{10,11},{11... | collective-permute-start | bytes 344072 | tf_op jit(solution)/shard_map/ppermute | solution.py:677
  6.4 1.9 %collective-permute-start.1 = (bf16[64,7,128]{2,1,0:T(8,128)(2,1)}, bf16[64,7,128]{2,1,0:T(8,128)(2,1)S(1)}, u32[]{:S(2)}, u32[]{:S(2)}) collective-permute-start(bf16[64,7,128]{2,1,0:T(8,128)(2,1)} %get-tuple-element.10), channel_id=1, source_target_pairs={{1,0},{2,1},{3,2},{4,3},{5,4},{6,5},{7,6},{9,8},{10,9},{11,10},{12... | collective-permute-start | bytes 344072 | tf_op jit(solution)/shard_map/ppermute | solution.py:678
  8.3 0.3 collective-permute-done.west_ref.refs_2_.refs_4_
  8.6 4.3 %collective-permute-done.1.east_ref.refs_3_.refs_5_ = bf16[64,7,128]{2,1,0:T(8,128)(2,1)S(1)} collective-permute-done((bf16[64,7,128]{2,1,0:T(8,128)(2,1)}, bf16[64,7,128]{2,1,0:T(8,128)(2,1)S(1)}, u32[]{:S(2)}, u32[]{:S(2)}) %collective-permute-start.1) | collective-permute-done | bytes 114720 | tf_op jit(solution)/shard_map/ppermute | solution.py:678
  12.9 1.6 %copy-done = bf16[64,128,128]{2,1,0:T(8,128)(2,1)S(1)} copy-done((bf16[64,128,128]{2,1,0:T(8,128)(2,1)S(1)}, bf16[64,128,128]{2,1,0:T(8,128)(2,1)}, u32[]{:S(2)}) %copy-start) | copy-done | bytes 2097176
  14.4 0.7 %copy-done.4 = s32[1,2]{1,0:T(1,128)S(1)} copy-done((s32[1,2]{1,0:T(1,128)S(1)}, s32[1,2]{1,0:T(1,128)}, u32[]{:S(2)}) %copy-start.4) | copy-done | bytes 32
  15.1 0.6 rim_rows.1
  15.7 1.3 %collective-permute-start.2 = (bf16[7,144,128]{2,1,0:T(8,128)(2,1)S(1)}, bf16[7,144,128]{2,1,0:T(8,128)(2,1)S(1)}, u32[]{:S(2)}, u32[]{:S(2)}) collective-permute-start(bf16[7,144,128]{2,1,0:T(8,128)(2,1)S(1)} %get-tuple-element.11), channel_id=1, source_target_pairs={{0,8},{8,16},{16,24},{24,0},{1,9},{9,17},{17,25},{25,1},{2,10},{10... | collective-permute-start | bytes 774152 | tf_op jit(solution)/shard_map/ppermute | solution.py:677
  17.0 1.2 %collective-permute-start.3 = (bf16[7,144,128]{2,1,0:T(8,128)(2,1)S(1)}, bf16[7,144,128]{2,1,0:T(8,128)(2,1)S(1)}, u32[]{:S(2)}, u32[]{:S(2)}) collective-permute-start(bf16[7,144,128]{2,1,0:T(8,128)(2,1)S(1)} %get-tuple-element.12), channel_id=1, source_target_pairs={{8,0},{16,8},{24,16},{0,24},{9,1},{17,9},{25,17},{1,25},{10,2},{18... | collective-permute-start | bytes 774152 | tf_op jit(solution)/shard_map/ppermute | solution.py:678
  18.1 0.7 %copy.10.conv_ref = bf16[2,7,7,128]{3,2,1,0:T(8,128)(2,1)S(1)} copy(bf16[2,7,7,128]{3,0,2,1:T(2,128)(2,1)} %param.11) | data formatting | bytes 50176 | tf_op args[2]
  18.9 2.2 %bands.2.refs_4_.refs_6_ = bf16[8,8,2,256,128]{4,3,2,1,0:T(8,128)(2,1)S(1)} custom-call(bf16[2,7,7,128]{3,2,1,0:T(8,128)(2,1)S(1)} %copy.10.conv_ref), custom_call_target="tpu_custom_call" | custom-call | flops 16777216 | bytes 8388608 | tf_op jit(solution)/shard_map/bands/pallas_call | solution.py:86
  21.1 0.0 copy-start.1
  21.1 0.0 copy-start.2
  21.1 0.0 copy-start.3
  21.2 0.0 copy-start.5
  21.2 0.0 copy-start.6
  21.2 0.0 copy-start.7
  21.2 0.0 copy-start.8
  21.2 0.0 copy-start.9
  21.2 2.2 %bands.3.refs_7_ = bf16[8,8,2,256,128]{4,3,2,1,0:T(8,128)(2,1)S(1)} custom-call(bf16[2,7,7,128]{3,2,1,0:T(8,128)(2,1)S(1)} %copy.10.conv_ref), custom_call_target="tpu_custom_call" | custom-call | flops 16777216 | bytes 8388608 | tf_op jit(solution)/shard_map/bands/pallas_call | solution.py:86
  23.5 0.0 copy-done.1
  23.5 0.0 copy-done.2
  23.5 0.0 copy-done.3
  23.5 0.0 copy-done.5
  23.5 0.0 copy-done.6
  23.5 0.0 copy-done.7
  23.5 0.0 copy-done.8
  23.6 14.1 %inner_blocks.1.refs_8_ = f32[48,168,128]{2,1,0:T(8,128)S(1)} custom-call(s32[1,2]{1,0:T(1,128)S(1)} %copy-done.5, bf16[64,128,128]{2,1,0:T(8,128)(2,1)S(1)} %copy-done.1, bf16[64,7,128]{2,1,0:T(8,128)(2,1)S(1)} %collective-permute-done.west_ref.refs_2_.refs_4_, bf16[64,7,128]{2,1,0:T(8,128)(2,1)S(1)} %collective-permute-done.1.east_ref.refs_3_.refs_5_, ...), custom_call_target="tpu_custom_call" | custom-call | flops 1966080000 | bytes 7864320 | tf_op jit(solution)/shard_map/inner_blocks/pallas_call | solution.py:623
  37.7 0.0 collective-permute-done.2.refs_2_
  37.7 0.0 collective-permute-done.3.refs_3_
  37.7 26.2 %outer_blocks.1 = bf16[64,128,128]{2,1,0:T(8,128)(2,1)} custom-call(s32[1,2]{1,0:T(1,128)S(1)} %copy-done.5, bf16[64,128,128]{2,1,0:T(8,128)(2,1)S(1)} %copy-done.1, bf16[7,144,128]{2,1,0:T(8,128)(2,1)S(1)} %collective-permute-done.2.refs_2_, bf16[7,144,128]{2,1,0:T(8,128)(2,1)S(1)} %collective-permute-done.3.refs_3_, ...), custom_call_target="tpu_custom_call" | custom-call | tf_op jit(solution)/shard_map/outer_blocks/pallas_call | solution.py:648
  (3 shorter events, 0.0 us)
Async XLA Ops:
  1.8 6.8 %collective-permute-start = (bf16[64,7,128]{2,1,0:T(8,128)(2,1)}, bf16[64,7,128]{2,1,0:T(8,128)(2,1)S(1)}, u32[]{:S(2)}, u32[]{:S(2)}) collective-permute-start(bf16[64,7,128]{2,1,0:T(8,128)(2,1)} %get-tuple-element.9), channel_id=1, source_target_pairs={{0,1},{1,2},{2,3},{3,4},{4,5},{5,6},{6,7},{8,9},{9,10},{10,11},{11... | collective-permute-start | bytes 344072 | tf_op jit(solution)/shard_map/ppermute | solution.py:677
  6.4 6.5 %collective-permute-start.1 = (bf16[64,7,128]{2,1,0:T(8,128)(2,1)}, bf16[64,7,128]{2,1,0:T(8,128)(2,1)S(1)}, u32[]{:S(2)}, u32[]{:S(2)}) collective-permute-start(bf16[64,7,128]{2,1,0:T(8,128)(2,1)} %get-tuple-element.10), channel_id=1, source_target_pairs={{1,0},{2,1},{3,2},{4,3},{5,4},{6,5},{7,6},{9,8},{10,9},{11,10},{12... | collective-permute-start | bytes 344072 | tf_op jit(solution)/shard_map/ppermute | solution.py:678
  12.8 1.6 %copy-start = (bf16[64,128,128]{2,1,0:T(8,128)(2,1)S(1)}, bf16[64,128,128]{2,1,0:T(8,128)(2,1)}, u32[]{:S(2)}) copy-start(bf16[64,128,128]{2,1,0:T(8,128)(2,1)} %refs_1_.3) | copy-start | bytes 6291460
  14.4 0.7 %copy-start.4 = (s32[1,2]{1,0:T(1,128)S(1)}, s32[1,2]{1,0:T(1,128)}, u32[]{:S(2)}) copy-start(s32[1,2]{1,0:T(1,128)} %refs_0_.3) | copy-start | bytes 28
  15.7 21.9 %collective-permute-start.2 = (bf16[7,144,128]{2,1,0:T(8,128)(2,1)S(1)}, bf16[7,144,128]{2,1,0:T(8,128)(2,1)S(1)}, u32[]{:S(2)}, u32[]{:S(2)}) collective-permute-start(bf16[7,144,128]{2,1,0:T(8,128)(2,1)S(1)} %get-tuple-element.11), channel_id=1, source_target_pairs={{0,8},{8,16},{16,24},{24,0},{1,9},{9,17},{17,25},{25,1},{2,10},{10... | collective-permute-start | bytes 774152 | tf_op jit(solution)/shard_map/ppermute | solution.py:677
  17.0 20.7 %collective-permute-start.3 = (bf16[7,144,128]{2,1,0:T(8,128)(2,1)S(1)}, bf16[7,144,128]{2,1,0:T(8,128)(2,1)S(1)}, u32[]{:S(2)}, u32[]{:S(2)}) collective-permute-start(bf16[7,144,128]{2,1,0:T(8,128)(2,1)S(1)} %get-tuple-element.12), channel_id=1, source_target_pairs={{8,0},{16,8},{24,16},{0,24},{9,1},{17,9},{25,17},{1,25},{10,2},{18... | collective-permute-start | bytes 774152 | tf_op jit(solution)/shard_map/ppermute | solution.py:678
  21.1 2.4 %copy-start.1 = (bf16[64,128,128]{2,1,0:T(8,128)(2,1)S(1)}, bf16[64,128,128]{2,1,0:T(8,128)(2,1)}, u32[]{:S(2)}) copy-start(bf16[64,128,128]{2,1,0:T(8,128)(2,1)} %refs_1_.3) | copy-start | bytes 6291460
  21.1 2.3 %copy-start.2 = (bf16[2,128,256]{2,1,0:T(8,128)(2,1)S(1)}, bf16[2,128,256]{2,1,0:T(8,128)(2,1)}, u32[]{:S(2)}) copy-start(bf16[2,128,256]{2,1,0:T(8,128)(2,1)} %refs_11_.1) | copy-start | bytes 393220
  21.1 2.3 %copy-start.3 = (bf16[2,256,128]{2,1,0:T(8,128)(2,1)S(1)}, bf16[2,256,128]{2,1,0:T(8,128)(2,1)}, u32[]{:S(2)}) copy-start(bf16[2,256,128]{2,1,0:T(8,128)(2,1)} %refs_13_.1) | copy-start | bytes 393220
  21.2 2.3 %copy-start.5 = (s32[1,2]{1,0:T(1,128)S(1)}, s32[1,2]{1,0:T(1,128)}, u32[]{:S(2)}) copy-start(s32[1,2]{1,0:T(1,128)} %refs_0_.3) | copy-start | bytes 28
  21.2 2.3 %copy-start.6 = (f32[2,256]{1,0:T(2,128)S(1)}, f32[2,256]{1,0:T(2,128)}, u32[]{:S(2)}) copy-start(f32[2,256]{1,0:T(2,128)} %refs_12_.1) | copy-start | bytes 6148
  21.2 2.3 %copy-start.7 = (f32[2,128]{1,0:T(2,128)S(1)}, f32[2,128]{1,0:T(2,128)}, u32[]{:S(2)}) copy-start(f32[2,128]{1,0:T(2,128)} %refs_9_.3) | copy-start | bytes 3076
  21.2 2.3 %copy-start.8 = (f32[2,128]{1,0:T(2,128)S(1)}, f32[2,128]{1,0:T(2,128)}, u32[]{:S(2)}) copy-start(f32[2,128]{1,0:T(2,128)} %refs_10_.3) | copy-start | bytes 3076
  21.2 2.3 %copy-start.9 = (f32[2,128]{1,0:T(2,128)S(1)}, f32[2,128]{1,0:T(2,128)}, u32[]{:S(2)}) copy-start(f32[2,128]{1,0:T(2,128)} %refs_14_.1) | copy-start | bytes 3076
where the time goes:
time: 64.1 us; the launch traced here: 63.8 us
  Pallas kernels  47.1 us (73%)
  starting transfers between devices  8.92 us (14%)
  waiting for transfers between devices  4.57 us (7%)
  local copies, waits for them, and re-layouts  3.04 us (5%)
    pallas_call x1, Pallas kernels, outer_call(): pl.pallas_call(in_kernel(outer_body, channels // SEG, height // PHASE_I +...  26.2 us
    pallas_call x1, Pallas kernels, inner_call(): pl.pallas_call(in_kernel(inner_body, channels // SEG, inner + 1, inner, s...  14.1 us
    ppermute x2, starting transfers between devices, shift_pair(): lax.ppermute(tail, axis, [(i, (i + 1) % count) for i in range(ends)])  5.85 us
    pallas_call x2, Pallas kernels, band_call(): pl.pallas_call(band_body, grid=(groups,), out_shape=jax.ShapeDtypeStruct(...  4.47 us
    ppermute x2, waiting for transfers between devices, shift_pair(): lax.ppermute(head, axis, [((i + 1) % count, i) for i in range(ends)])  4.26 us
    ppermute x2, starting transfers between devices, shift_pair(): lax.ppermute(head, axis, [((i + 1) % count, i) for i in range(ends)])  3.07 us
    unnamed x21, local copies, waits for them, and re-layouts  3.04 us
    pallas_call x1, Pallas kernels, rim_cols_call(): pl.pallas_call(functools.partial(rim_cols_body, tile=tile), out_shape=[sh...  1.75 us
  transfers between devices with their start and end apart: 4, of which 2 were waited for; matrix products, arithmetic and copies ran while one was open for 1% of the time, Pallas kernels for 29%

commit v1 on v0

--- a/solution.py
+++ b/solution.py
@@ -45,14 +45,14 @@
     return ((high * 2 + p2 + (g & (1 - p1))) & 3) * 2 + p1
 
 
-def band_body(conv_ref, band_ref, taps_ref, rows_ref):
+def band_body(conv_ref, band_ref, taps_ref, rows_ref, *, layer):
     f32 = jnp.float32
     g = pl.program_id(0)
 
     @pl.when(g == 0)
     def _():
         taps_ref[...] = jnp.zeros(taps_ref.shape, f32)
-        taps_ref[7:14, 8:15, :] = conv_ref[...].astype(f32)
+        taps_ref[7:14, 8:15, :] = conv_ref[:, :, layer, :].astype(f32)
 
         def tap_rows(q, carry):
             for half in range(2):
@@ -84,10 +84,10 @@
 def band_call(kernels, layer):
     groups = kernels.shape[3] // SEG
     return pl.pallas_call(
-        band_body,
+        functools.partial(band_body, layer=layer),
         grid=(groups,),
         out_shape=jax.ShapeDtypeStruct((groups, CHUNKS, 2, WIDE, LANES), jnp.bfloat16),
-        in_specs=[pl.BlockSpec((None,) + kernels.shape[1:], lambda g: (layer, 0, 0, 0))],
+        in_specs=[pl.BlockSpec(kernels.shape, lambda g: (0, 0, 0, 0))],
         out_specs=pl.BlockSpec((1, CHUNKS, 2, WIDE, LANES), lambda g: (g, 0, 0, 0, 0)),
         scratch_shapes=[
             pltpu.VMEM((24, 24, LANES), jnp.float32),
@@ -149,9 +149,26 @@
     )(wet, state)
 
 
-def rim_rows_body(wet_ref, state_ref, west_ref, east_ref, head_ref, tail_ref, *, tile):
+def rim_rows_body(
+    wet_ref,
+    state_ref,
+    west_in_ref,
+    east_in_ref,
+    head_ref,
+    tail_ref,
+    west_ref,
+    east_ref,
+    *,
+    tile,
+):
     f32 = jnp.float32
     bf16 = jnp.bfloat16
+    place = lax.axis_index("lat")
+    for in_ref, clean_ref, inside in (
+        (west_in_ref, west_ref, place > 0),
+        (east_in_ref, east_ref, place < lax.axis_size("lat") - 1),
+    ):
+        clean_ref[...] = jnp.where(inside, in_ref[...].astype(f32), 0.0).astype(bf16)
     height, width, channels = state_ref.shape
     for out_ref, ti, first in ((head_ref, 0, 0), (tail_ref, wet_ref.shape[0] - 1, height - RIM)):
         out_ref[:, 0:LEFT, :] = jnp.zeros((RIM + 1, LEFT, channels), bf16)
@@ -179,9 +196,9 @@
     vmem = pl.BlockSpec(memory_space=pltpu.VMEM)
     return pl.pallas_call(
         functools.partial(rim_rows_body, tile=tile),
-        out_shape=[shape, shape],
+        out_shape=[shape, shape] + [jax.ShapeDtypeStruct(west.shape, west.dtype)] * 2,
         in_specs=[pl.BlockSpec(memory_space=pltpu.SMEM)] + [vmem] * 3,
-        out_specs=[vmem, vmem],
+        out_specs=[vmem] * 4,
         compiler_params=pltpu.CompilerParams(vmem_limit_bytes=8 << 20),
         name="rim_rows",
     )(wet, state, west, east)
@@ -325,7 +342,7 @@
             ].reshape(blocks, pairs, STRIPS, LANES)
         return carry
 
-    lax.fori_loop(0, groups, convolve, 0, unroll=4)
+    lax.fori_loop(0, groups, convolve, 0, unroll=8)
 
     def to_cells(blk):
         for v in range(pairs):
@@ -374,7 +391,7 @@
     to_cells(0)
     normalize()
     to_cells(1)
-    lax.fori_loop(0, blocks, mix, 0)
+    lax.fori_loop(0, blocks, mix, 0, unroll=2)
     if finish is not None:
         finish(blocks - 1)
 
@@ -671,11 +688,10 @@
     )(wet, state, top, bottom, west, east, *bands, part, *weights)
 
 
-def shift_pair(head, tail, axis, closed):
+def shift_pair(head, tail, axis):
     count = lax.axis_size(axis)
-    ends = count if closed else count - 1
-    before = lax.ppermute(tail, axis, [(i, (i + 1) % count) for i in range(ends)])
-    after = lax.ppermute(head, axis, [((i + 1) % count, i) for i in range(ends)])
+    before = lax.ppermute(tail, axis, [(i, (i + 1) % count) for i in range(count)])
+    after = lax.ppermute(head, axis, [((i + 1) % count, i) for i in range(count)])
     return before, after
 
 
@@ -692,12 +708,13 @@
 ):
     tile = ocean_field.shape[0] // wet_tiles.shape[0]
     cols = rim_cols_call(wet_tiles, ocean_field, tile)
-    west, east = shift_pair(*cols, "lat", False)
-    rows = rim_rows_call(wet_tiles, ocean_field, west, east, tile)
-    top, bottom = shift_pair(*rows, "lon", True)
+    west, east = shift_pair(*cols, "lat")
+    *rows, west, east = rim_rows_call(wet_tiles, ocean_field, west, east, tile)
+    top, bottom = shift_pair(*rows, "lon")
     bands = []
+    kernels = jnp.transpose(conv_weight, (1, 2, 0, 3))
     for layer in range(conv_weight.shape[0]):
-        bands.append(band_call(conv_weight, layer))
+        bands.append(band_call(kernels, layer))
     weights = (norm_gain, norm_bias, inner_weight, inner_bias, outer_weight, outer_bias)
     part = inner_call(wet_tiles, ocean_field, west, east, bands[0], weights, tile)
     return outer_call(wet_tiles, ocean_field, top, bottom, west, east, bands, part, weights, tile)

time: 64.1 us -> 59 us (0.920)
  starting transfers between devices: 8.92 us -> 5.51 us
  Pallas kernels: 47.1 us -> 44.5 us
  waiting for transfers between devices: 4.57 us -> 5.44 us
    ppermute x4, starting transfers between devices: 8.92 us -> 5.51 us  [the longest x2 4.49 us: shift_pair(): lax.ppermute(tail, axis, [(i, (i + 1) % count) for i in range(count)])]
    pallas_call x1, Pallas kernels: 26.2 us -> 24.3 us  [outer_call(): pl.pallas_call(in_kernel(outer_body, channels // SEG, height // PHASE_I +...]
    pallas_call x1, Pallas kernels: 14.1 us -> 13.2 us  [inner_call(): pl.pallas_call(in_kernel(inner_body, channels // SEG, inner + 1, inner, s...]
    ppermute x4, waiting for transfers between devices: 4.57 us -> 5.44 us  [the longest x2 3.18 us: shift_pair(): lax.ppermute(head, axis, [((i + 1) % count, i) for i in range(count)])]
    unnamed x21 -> x22, local copies, waits for them, and re-layouts: 3.04 us -> 3.03 us
  transfers between devices with their start and end apart: 4 -> 4, of which waited for: 2 -> 2; matrix products, arithmetic and copies ran while one was open for 1% -> 0% of each run, Pallas kernels for 29% -> 30%
where the time goes in v1:
time: 59 us; the launch traced here: 58.8 us
  Pallas kernels  44.5 us (75%)
  starting transfers between devices  5.51 us (9%)
  waiting for transfers between devices  5.44 us (9%)
  local copies, waits for them, and re-layouts  3.03 us (5%)
    pallas_call x1, Pallas kernels, outer_call(): pl.pallas_call(in_kernel(outer_body, channels // SEG, height // PHASE_I +...  24.3 us
    pallas_call x1, Pallas kernels, inner_call(): pl.pallas_call(in_kernel(inner_body, channels // SEG, inner + 1, inner, s...  13.2 us
    pallas_call x2, Pallas kernels, band_call(): pl.pallas_call(functools.partial(band_body, layer=layer), grid=(groups,),...  4.5 us
    ppermute x2, starting transfers between devices, shift_pair(): lax.ppermute(tail, axis, [(i, (i + 1) % count) for i in range(count)])  4.49 us
    ppermute x2, waiting for transfers between devices, shift_pair(): lax.ppermute(head, axis, [((i + 1) % count, i) for i in range(count)])  3.18 us
    unnamed x22, local copies, waits for them, and re-layouts  3.03 us
    ppermute x2, waiting for transfers between devices, shift_pair(): lax.ppermute(tail, axis, [(i, (i + 1) % count) for i in range(count)])  2.26 us
    pallas_call x1, Pallas kernels, rim_cols_call(): pl.pallas_call(functools.partial(rim_cols_body, tile=tile), out_shape=[sh...  1.75 us
  transfers between devices with their start and end apart: 4, of which 2 were waited for; matrix products, arithmetic and copies ran while one was open for 0% of the time, Pallas kernels for 30%

profile of v1, /device:TPU:1, one launch (start us, length us, event | category | flops | bytes accessed | tf_op | source)
XLA Modules:
  0.0 58.8 jit_solution(15185404201863660332)
XLA Ops:
  0.0 1.8 %rim_cols.1 = (bf16[64,7,128]{2,1,0:T(8,128)(2,1)}, bf16[64,7,128]{2,1,0:T(8,128)(2,1)}) custom-call(s32[1,2]{1,0:T(1,128)} %refs_0_.3, bf16[64,128,128]{2,1,0:T(8,128)(2,1)} %refs_1_.3), custom_call_target="tpu_custom_call" | custom-call | tf_op jit(solution)/shard_map/rim_cols/pallas_call | solution.py:136
  1.8 2.7 %collective-permute-start = (bf16[64,7,128]{2,1,0:T(8,128)(2,1)}, bf16[64,7,128]{2,1,0:T(8,128)(2,1)S(1)}, u32[]{:S(2)}, u32[]{:S(2)}) collective-permute-start(bf16[64,7,128]{2,1,0:T(8,128)(2,1)} %get-tuple-element.11), channel_id=1, source_target_pairs={{0,1},{1,2},{2,3},{3,4},{4,5},{5,6},{6,7},{7,0},{8,9},{9,10},{10,1... | collective-permute-start | bytes 344072 | tf_op jit(solution)/shard_map/ppermute | solution.py:693
  4.5 0.0 collective-permute-start.1
  4.5 2.3 %collective-permute-done.west_in_ref = bf16[64,7,128]{2,1,0:T(8,128)(2,1)S(1)} collective-permute-done((bf16[64,7,128]{2,1,0:T(8,128)(2,1)}, bf16[64,7,128]{2,1,0:T(8,128)(2,1)S(1)}, u32[]{:S(2)}, u32[]{:S(2)}) %collective-permute-start) | collective-permute-done | bytes 114720 | tf_op jit(solution)/shard_map/ppermute | solution.py:693
  6.8 3.2 %collective-permute-done.1.east_in_ref = bf16[64,7,128]{2,1,0:T(8,128)(2,1)S(1)} collective-permute-done((bf16[64,7,128]{2,1,0:T(8,128)(2,1)}, bf16[64,7,128]{2,1,0:T(8,128)(2,1)S(1)}, u32[]{:S(2)}, u32[]{:S(2)}) %collective-permute-start.1) | collective-permute-done | bytes 114720 | tf_op jit(solution)/shard_map/ppermute | solution.py:694
  9.9 1.6 %copy-done = bf16[64,128,128]{2,1,0:T(8,128)(2,1)S(1)} copy-done((bf16[64,128,128]{2,1,0:T(8,128)(2,1)S(1)}, bf16[64,128,128]{2,1,0:T(8,128)(2,1)}, u32[]{:S(2)}) %copy-start) | copy-done | bytes 2097176
  11.5 0.7 %copy-done.5 = s32[1,2]{1,0:T(1,128)S(1)} copy-done((s32[1,2]{1,0:T(1,128)S(1)}, s32[1,2]{1,0:T(1,128)}, u32[]{:S(2)}) %copy-start.5) | copy-done | bytes 32
  12.2 0.7 %rim_rows.1 = (bf16[7,144,128]{2,1,0:T(8,128)(2,1)S(1)}, bf16[7,144,128]{2,1,0:T(8,128)(2,1)S(1)}, bf16[64,7,128]{2,1,0:T(8,128)(2,1)S(1)}, bf16[64,7,128]{2,1,0:T(8,128)(2,1)S(1)}) custom-call(s32[1,2]{1,0:T(1,128)S(1)} %copy-done.5, bf16[64,128,128]{2,1,0:T(8,128)(2,1)S(1)} %copy-done, bf16[64,7,128]{2,1,0:T(8,128)(2,1)S(1)} %collective-permute-done.west_in_ref, ...), custom_call_target="tpu_custom_call" | custom-call | tf_op jit(solution)/shard_map/rim_rows/pallas_call | solution.py:197
  12.9 1.8 %collective-permute-start.2 = (bf16[7,144,128]{2,1,0:T(8,128)(2,1)S(1)}, bf16[7,144,128]{2,1,0:T(8,128)(2,1)S(1)}, u32[]{:S(2)}, u32[]{:S(2)}) collective-permute-start(bf16[7,144,128]{2,1,0:T(8,128)(2,1)S(1)} %get-tuple-element.13), channel_id=1, source_target_pairs={{0,8},{8,16},{16,24},{24,0},{1,9},{9,17},{17,25},{25,1},{2,10},{10... | collective-permute-start | bytes 774152 | tf_op jit(solution)/shard_map/ppermute | solution.py:693
  14.6 1.0 %collective-permute-start.3 = (bf16[7,144,128]{2,1,0:T(8,128)(2,1)S(1)}, bf16[7,144,128]{2,1,0:T(8,128)(2,1)S(1)}, u32[]{:S(2)}, u32[]{:S(2)}) collective-permute-start(bf16[7,144,128]{2,1,0:T(8,128)(2,1)S(1)} %get-tuple-element.14), channel_id=1, source_target_pairs={{8,0},{16,8},{24,16},{0,24},{9,1},{17,9},{25,17},{1,25},{10,2},{18... | collective-permute-start | bytes 774152 | tf_op jit(solution)/shard_map/ppermute | solution.py:694
  15.7 0.7 %copy-done.4 = bf16[2,7,7,128]{3,0,2,1:T(2,128)(2,1)S(1)} copy-done((bf16[2,7,7,128]{3,0,2,1:T(2,128)(2,1)S(1)}, bf16[2,7,7,128]{3,0,2,1:T(2,128)(2,1)}, u32[]{:S(2)}) %copy-start.4) | copy-done | bytes 25112
  16.4 2.2 %bands.2.refs_4_.refs_6_ = bf16[8,8,2,256,128]{4,3,2,1,0:T(8,128)(2,1)S(1)} custom-call(bf16[7,7,2,128]{3,2,1,0:T(2,128)(2,1)S(1)} %bitcast.1), custom_call_target="tpu_custom_call" | custom-call | flops 16777216 | bytes 8388608 | tf_op jit(solution)/shard_map/bands/pallas_call | solution.py:86
  18.7 0.0 copy-start.1
  18.7 0.0 copy-start.2
  18.7 0.0 copy-start.3
  18.7 0.0 copy-start.6
  18.7 0.0 copy-start.7
  18.7 0.0 copy-start.8
  18.7 0.0 copy-start.9
  18.7 0.0 copy-start.10
  18.8 2.3 %bands.3.refs_7_ = bf16[8,8,2,256,128]{4,3,2,1,0:T(8,128)(2,1)S(1)} custom-call(bf16[7,7,2,128]{3,2,1,0:T(2,128)(2,1)S(1)} %bitcast.2), custom_call_target="tpu_custom_call" | custom-call | flops 16777216 | bytes 8388608 | tf_op jit(solution)/shard_map/bands/pallas_call | solution.py:86
  21.0 0.0 copy-done.1
  21.0 0.0 copy-done.2
  21.0 0.0 copy-done.3
  21.1 0.0 copy-done.6
  21.1 0.0 copy-done.7
  21.1 0.0 copy-done.8
  21.1 0.0 copy-done.9
  21.1 13.2 %inner_blocks.1.refs_8_ = f32[48,168,128]{2,1,0:T(8,128)S(1)} custom-call(s32[1,2]{1,0:T(1,128)S(1)} %copy-done.6, bf16[64,128,128]{2,1,0:T(8,128)(2,1)S(1)} %copy-done.1, bf16[64,7,128]{2,1,0:T(8,128)(2,1)S(1)} %get-tuple-element.15.refs_2_.refs_4_, bf16[64,7,128]{2,1,0:T(8,128)(2,1)S(1)} %get-tuple-element.16.refs_3_.refs_5_, ...), custom_call_target="tpu_custom_call" | custom-call | flops 1966080000 | bytes 7864320 | tf_op jit(solution)/shard_map/inner_blocks/pallas_call | solution.py:640
  34.3 0.0 collective-permute-done.2.refs_2_
  34.3 0.0 collective-permute-done.3.refs_3_
  34.3 24.3 %outer_blocks.1 = bf16[64,128,128]{2,1,0:T(8,128)(2,1)} custom-call(s32[1,2]{1,0:T(1,128)S(1)} %copy-done.6, bf16[64,128,128]{2,1,0:T(8,128)(2,1)S(1)} %copy-done.1, bf16[7,144,128]{2,1,0:T(8,128)(2,1)S(1)} %collective-permute-done.2.refs_2_, bf16[7,144,128]{2,1,0:T(8,128)(2,1)S(1)} %collective-permute-done.3.refs_3_, ...), custom_call_target="tpu_custom_call" | custom-call | tf_op jit(solution)/shard_map/outer_blocks/pallas_call | solution.py:665
  (4 shorter events, 0.0 us)
Async XLA Ops:
  1.8 5.0 %collective-permute-start = (bf16[64,7,128]{2,1,0:T(8,128)(2,1)}, bf16[64,7,128]{2,1,0:T(8,128)(2,1)S(1)}, u32[]{:S(2)}, u32[]{:S(2)}) collective-permute-start(bf16[64,7,128]{2,1,0:T(8,128)(2,1)} %get-tuple-element.11), channel_id=1, source_target_pairs={{0,1},{1,2},{2,3},{3,4},{4,5},{5,6},{6,7},{7,0},{8,9},{9,10},{10,1... | collective-permute-start | bytes 344072 | tf_op jit(solution)/shard_map/ppermute | solution.py:693
  4.5 5.4 %collective-permute-start.1 = (bf16[64,7,128]{2,1,0:T(8,128)(2,1)}, bf16[64,7,128]{2,1,0:T(8,128)(2,1)S(1)}, u32[]{:S(2)}, u32[]{:S(2)}) collective-permute-start(bf16[64,7,128]{2,1,0:T(8,128)(2,1)} %get-tuple-element.12), channel_id=1, source_target_pairs={{1,0},{2,1},{3,2},{4,3},{5,4},{6,5},{7,6},{0,7},{9,8},{10,9},{11,1... | collective-permute-start | bytes 344072 | tf_op jit(solution)/shard_map/ppermute | solution.py:694
  9.9 1.6 %copy-start = (bf16[64,128,128]{2,1,0:T(8,128)(2,1)S(1)}, bf16[64,128,128]{2,1,0:T(8,128)(2,1)}, u32[]{:S(2)}) copy-start(bf16[64,128,128]{2,1,0:T(8,128)(2,1)} %refs_1_.3) | copy-start | bytes 6291460
  11.5 0.7 %copy-start.5 = (s32[1,2]{1,0:T(1,128)S(1)}, s32[1,2]{1,0:T(1,128)}, u32[]{:S(2)}) copy-start(s32[1,2]{1,0:T(1,128)} %refs_0_.3) | copy-start | bytes 28
  12.9 21.4 %collective-permute-start.2 = (bf16[7,144,128]{2,1,0:T(8,128)(2,1)S(1)}, bf16[7,144,128]{2,1,0:T(8,128)(2,1)S(1)}, u32[]{:S(2)}, u32[]{:S(2)}) collective-permute-start(bf16[7,144,128]{2,1,0:T(8,128)(2,1)S(1)} %get-tuple-element.13), channel_id=1, source_target_pairs={{0,8},{8,16},{16,24},{24,0},{1,9},{9,17},{17,25},{25,1},{2,10},{10... | collective-permute-start | bytes 774152 | tf_op jit(solution)/shard_map/ppermute | solution.py:693
  14.6 19.7 %collective-permute-start.3 = (bf16[7,144,128]{2,1,0:T(8,128)(2,1)S(1)}, bf16[7,144,128]{2,1,0:T(8,128)(2,1)S(1)}, u32[]{:S(2)}, u32[]{:S(2)}) collective-permute-start(bf16[7,144,128]{2,1,0:T(8,128)(2,1)S(1)} %get-tuple-element.14), channel_id=1, source_target_pairs={{8,0},{16,8},{24,16},{0,24},{9,1},{17,9},{25,17},{1,25},{10,2},{18... | collective-permute-start | bytes 774152 | tf_op jit(solution)/shard_map/ppermute | solution.py:694
  15.7 0.7 %copy-start.4 = (bf16[2,7,7,128]{3,0,2,1:T(2,128)(2,1)S(1)}, bf16[2,7,7,128]{3,0,2,1:T(2,128)(2,1)}, u32[]{:S(2)}) copy-start(bf16[2,7,7,128]{3,0,2,1:T(2,128)(2,1)} %param.11) | copy-start | bytes 75268
  18.7 2.4 %copy-start.1 = (bf16[64,128,128]{2,1,0:T(8,128)(2,1)S(1)}, bf16[64,128,128]{2,1,0:T(8,128)(2,1)}, u32[]{:S(2)}) copy-start(bf16[64,128,128]{2,1,0:T(8,128)(2,1)} %refs_1_.3) | copy-start | bytes 6291460
  18.7 2.4 %copy-start.2 = (bf16[2,128,256]{2,1,0:T(8,128)(2,1)S(1)}, bf16[2,128,256]{2,1,0:T(8,128)(2,1)}, u32[]{:S(2)}) copy-start(bf16[2,128,256]{2,1,0:T(8,128)(2,1)} %refs_11_.1) | copy-start | bytes 393220
  18.7 2.4 %copy-start.3 = (bf16[2,256,128]{2,1,0:T(8,128)(2,1)S(1)}, bf16[2,256,128]{2,1,0:T(8,128)(2,1)}, u32[]{:S(2)}) copy-start(bf16[2,256,128]{2,1,0:T(8,128)(2,1)} %refs_13_.1) | copy-start | bytes 393220
  18.7 2.4 %copy-start.6 = (s32[1,2]{1,0:T(1,128)S(1)}, s32[1,2]{1,0:T(1,128)}, u32[]{:S(2)}) copy-start(s32[1,2]{1,0:T(1,128)} %refs_0_.3) | copy-start | bytes 28
  18.7 2.4 %copy-start.7 = (f32[2,256]{1,0:T(2,128)S(1)}, f32[2,256]{1,0:T(2,128)}, u32[]{:S(2)}) copy-start(f32[2,256]{1,0:T(2,128)} %refs_12_.1) | copy-start | bytes 6148
  18.7 2.4 %copy-start.8 = (f32[2,128]{1,0:T(2,128)S(1)}, f32[2,128]{1,0:T(2,128)}, u32[]{:S(2)}) copy-start(f32[2,128]{1,0:T(2,128)} %refs_9_.3) | copy-start | bytes 3076
  18.7 2.4 %copy-start.9 = (f32[2,128]{1,0:T(2,128)S(1)}, f32[2,128]{1,0:T(2,128)}, u32[]{:S(2)}) copy-start(f32[2,128]{1,0:T(2,128)} %refs_10_.3) | copy-start | bytes 3076
  18.7 2.4 %copy-start.10 = (f32[2,128]{1,0:T(2,128)S(1)}, f32[2,128]{1,0:T(2,128)}, u32[]{:S(2)}) copy-start(f32[2,128]{1,0:T(2,128)} %refs_14_.1) | copy-start | bytes 3076
